TPU v7x, 512 devices: a whole 4x4x16 slice. The times are simulated.
512 devices in a mesh: dp: 32 (over z, core), tensor: 16 (over y, x).
Axes of the slice: x: 4, y: 4, z: 16, core: 2. Of those that a mesh axis runs over, the one named last changes fastest.
Arguments:
- features: bfloat16 [40960, 2048], P(('dp', 'tensor')), may hold values from -6 to 6
- w_hidden: bfloat16 [2048, 2048], P(None, 'tensor'), may hold values from -0.125 to 0.125
- w_embed: bfloat16 [2048, 768], P('tensor'), may hold values from -0.125 to 0.125
- members: bfloat16 [32, 2048, 768], P('dp', 'tensor'), may hold values from -6 to 6
- doc_owner: int32 [40960, 1], P('dp'), may hold values from 0 to 31; in each aligned block of 80 rows (0 to 79, 80 to 159, ...) at most 5 rows name the same one
- doc_local: int32 [40960], P('dp'), may hold values from 0 to 15
- member_cluster: int32 [32, 2048], P('dp', 'tensor'), may hold values from 0 to 15, never falling along the last dimension, each value on 1 to 192 neighbouring positions
- member_valid: int32 [32, 2048], P('dp', 'tensor'), may hold values 0 or 1
Outputs:
- best: float32 [40960], P(('dp', 'tensor'))
Inputs may be any that keep to these rules, and one draw needn't show every extreme that they name: Among the 80 documents of one device (aligned blocks of doc_owner's rows, in the order of dp then tensor) no owner is named more than 5 times; some owner is named exactly 5 times. `member_cluster`: along each owner's row the clusters never fall; every cluster has 1 to 192 slots.
All inputs are finite; a program needn't handle non-finite values. No bound on the sum of `member_valid` on one device may be relied on, other than what follows from the above.
Results may differ from a plain program's by a relative error of at most 0.013.
Values may be sent and summed in bfloat16 or wider, within the bound.
No kernel may reach another device: no remote copies, remote signals or barrier semaphores. Data moves between devices by JAX's collectives and lax.ppermute only.
A program may use at most 64 MiB of HBM per device.

v0:
```python
import jax
import jax.numpy as jnp
from jax import lax
from jax.sharding import PartitionSpec as P

epsilon = 1e-06


def unit_rows(vectors):
    values = vectors.astype(jnp.float32)
    return (values / jnp.sqrt(jnp.sum(values * values, axis=-1, keepdims=True) + epsilon)).astype(
        jnp.bfloat16
    )


def slot_of(owner, owners_count, slot_cap):
    onehot = (owner[:, None] == jnp.arange(owners_count, dtype=jnp.int32)[None, :]).astype(
        jnp.int32
    )
    ranking = jnp.sum((jnp.cumsum(onehot, axis=0) - 1) * onehot, axis=1)
    return owner * slot_cap + ranking


def pack_rows(query, local, slot_index, slot_total):
    placing = slot_index[None, :] == jnp.arange(slot_total, dtype=jnp.int32)[:, None]
    outgoing = jnp.dot(
        placing.astype(jnp.bfloat16), query, preferred_element_type=jnp.float32
    ).astype(jnp.bfloat16)
    slot_tag = jnp.sum(jnp.where(placing, local[None, :] + 1, 0), axis=1)
    return (outgoing, slot_tag)


def best_scores(arrived, arrived_tag, unit, cluster_here, valid_here):
    scores = lax.dot_general(
        arrived, unit, (((1,), (1,)), ((), ())), preferred_element_type=jnp.float32
    )
    allowed = (valid_here[None, :] == 1) & (cluster_here[None, :] == arrived_tag[:, None] - 1)
    return jnp.max(jnp.where(allowed, scores, -1.0), axis=1)


def body(features, w_hidden, w_embed, members, doc_owner, doc_local, member_cluster, member_valid):
    owners_count = lax.axis_size("dp")
    tensor_index = lax.axis_index("tensor")
    row_total = features.shape[0]
    slot_cap = min(row_total, max(2, 2 * row_total // owners_count))
    hidden = jax.nn.gelu(
        jnp.dot(
            lax.all_gather(features, "tensor", axis=0, tiled=True),
            w_hidden,
            preferred_element_type=jnp.float32,
        )
    ).astype(jnp.bfloat16)
    unit = unit_rows(members.reshape(members.shape[1], members.shape[2]))
    cluster_here = member_cluster.reshape(-1)
    valid_here = member_valid.reshape(-1)
    owner_all = doc_owner[:, 0]
    summed = lax.psum_scatter(
        jnp.dot(hidden, w_embed, preferred_element_type=jnp.float32).astype(jnp.bfloat16),
        "tensor",
        scatter_dimension=0,
        tiled=True,
    ).astype(jnp.float32)
    query = unit_rows(summed)
    owner = lax.dynamic_slice_in_dim(owner_all, tensor_index * row_total, row_total, 0)
    local = lax.dynamic_slice_in_dim(doc_local, tensor_index * row_total, row_total, 0)
    slot_total = owners_count * slot_cap
    slot_index = slot_of(owner, owners_count, slot_cap)
    outgoing, slot_tag = pack_rows(query, local, slot_index, slot_total)
    arrived, arrived_tag = (
        lax.all_to_all(outgoing, "dp", split_axis=0, concat_axis=0, tiled=True),
        lax.all_to_all(slot_tag, "dp", split_axis=0, concat_axis=0, tiled=True),
    )
    shared, shared_tag = (
        lax.all_gather(arrived, "tensor", axis=0, tiled=True),
        lax.all_gather(arrived_tag, "tensor", axis=0, tiled=True),
    )
    partial_value = best_scores(shared, shared_tag, unit, cluster_here, valid_here)
    merged = lax.pmax(partial_value, "tensor")
    own_best = lax.dynamic_slice_in_dim(merged, tensor_index * slot_total, slot_total, 0)
    answers = lax.all_to_all(own_best, "dp", split_axis=0, concat_axis=0, tiled=True)
    return jnp.take(answers, slot_index, axis=0)


def solution(mesh):
    return jax.shard_map(
        body,
        mesh=mesh,
        in_specs=(
            P(("dp", "tensor"), None),
            P(None, "tensor"),
            P("tensor", None),
            P("dp", "tensor", None),
            P("dp", None),
            P("dp"),
            P("dp", "tensor"),
            P("dp", "tensor"),
        ),
        out_specs=P(("dp", "tensor")),
        check_vma=False,
    )
```

profile of v0, /device:TPU:1, one launch (start us, length us, event | category | flops | bytes accessed | tf_op | source)
XLA Modules:
  0.0 418.8 jit_solution(9117724124348048883)
XLA Ops:
  6.5 0.7 all-gather.3.cloned.1.call-update
  7.3 80.1 %all-gather.3.cloned.1.call-done = bf16[1280,2048]{1,0:T(8,128)(2,1)} async-done(((bf16[80,2048]{1,0:T(8,128)(2,1)}), bf16[1280,2048]{1,0:T(8,128)(2,1)}) %all-gather.3.cloned.1.call-update) | async-done | bytes 5242896 | tf_op jit(solution)/shard_map/all_gather | solution.py:48
  87.4 6.7 %convolution_convert_fusion = bf16[1280,768]{1,0:T(8,128)(2,1)} fusion(bf16[128,768]{1,0:T(8,128)(2,1)} %param.10, bf16[1280,2048]{1,0:T(8,128)(2,1)} %all-gather.3.cloned.1.call-done, bf16[2048,128]{1,0:T(8,128)(2,1)S(1)} %copy-done), kind=kOutput, calls=%fused_computation.2 | convolution fusion | flops 925204480 | bytes 7929856 | tf_op jit(solution)/shard_map/dot_general | solution.py:58
  94.2 0.8 fusion.25
  95.0 0.1 reduce_window_sum.11
  95.1 0.2 select_reduce_fusion.1
  95.3 0.8 multiply_add_fusion
  96.1 85.9 %reduce-scatter.2.cloned.1.call-done = bf16[80,768]{1,0:T(8,128)(2,1)} async-done(((bf16[1280,768]{1,0:T(8,128)(2,1)}), bf16[80,768]{1,0:T(8,128)(2,1)}) %reduce-scatter.2.cloned.1.call-update) | async-done | bytes 122896 | tf_op jit(solution)/shard_map/reduce_scatter | solution.py:57
  182.0 1.0 fusion.16
  183.0 1.2 convolution_convert_fusion.1
  184.3 42.5 %all_to_all.36 = bf16[32,5,768]{2,1,0:T(8,128)(2,1)S(1)} all-to-all(bf16[32,5,768]{2,1,0:T(8,128)(2,1)S(1)} %all_to_all.27), channel_id=1, replica_groups=mesh['dp'=32,'tensor'=16] {'dp'}, dimensions={0} | all-to-all | bytes 491520 | tf_op jit(solution)/shard_map/all_to_all | solution.py:70
  226.8 0.8 all_to_all.29
  227.6 0.8 dynamic-slice_add_fusion
  228.5 0.7 all_to_all.24
  229.3 3.9 all-to-all-start
  233.2 0.1 fusion.9
  233.3 0.8 compare_select_fusion
  234.1 1.3 dynamic-slice.1
  236.0 9.0 %all-to-all-done = s32[32,5,1]{1,2,0:T(1,128)S(1)} async-done(((s32[32,5,1]{1,2,0:T(1,128)}), s32[32,5,1]{1,2,0:T(1,128)S(1)}, u32[]{:S(2)}, u32[]{:S(2)}) %all-to-all-start) | async-done | bytes 672 | tf_op jit(solution)/shard_map/all_to_all | solution.py:71
  245.0 0.5 broadcast.54
  245.5 0.7 reduce.6
  246.3 0.3 dynamic-update-slice
  246.6 58.3 %all-reduce = s32[2560]{0:T(1024)S(1)} all-reduce(s32[2560]{0:T(1024)S(1)} %dynamic-update-slice), channel_id=1, replica_groups=mesh['dp'=32,'tensor'=16] {'tensor'}, use_global_device_ids=true, to_apply=%add | all-reduce | flops 2560 | bytes 20480
  304.9 3.5 fusion
  308.5 55.9 %pmax.7 = f32[2560]{0:T(1024)S(1)} all-reduce(f32[2560]{0:T(1024)S(1)} %fusion), channel_id=1, replica_groups=mesh['dp'=32,'tensor'=16] {'tensor'}, use_global_device_ids=true, to_apply=%region_7.8 | all-reduce | flops 2560 | bytes 20480 | tf_op jit(solution)/shard_map/pmax | solution.py:78
  364.5 0.7 all_to_all.30
  365.2 32.1 %all-to-all-start.2 = ((f32[32,5,1]{1,2,0:T(1,128)}), f32[32,5,1]{1,2,0:T(1,128)S(1)}, u32[]{:S(2)}, u32[]{:S(2)}) async-start(f32[32,5,1]{1,2,0:T(1,128)} %bitcast.9), calls=%async_computation.3 | async-start | bytes 32768 | tf_op jit(solution)/shard_map/all_to_all | solution.py:80
  397.3 11.9 %all-to-all-done.2 = f32[32,5,1]{1,2,0:T(1,128)S(1)} async-done(((f32[32,5,1]{1,2,0:T(1,128)}), f32[32,5,1]{1,2,0:T(1,128)S(1)}, u32[]{:S(2)}, u32[]{:S(2)}) %all-to-all-start.2) | async-done | bytes 672 | tf_op jit(solution)/shard_map/all_to_all | solution.py:80
  409.2 0.5 broadcast.55
  409.7 0.7 reduce.7
  410.5 1.3 gather_fusion
  411.7 0.5 bitcast_select_fusion
  (26 shorter events, 0.7 us)
Async XLA Ops:
  6.5 80.9 %copy-start = (bf16[2048,128]{1,0:T(8,128)(2,1)S(1)}, bf16[2048,128]{1,0:T(8,128)(2,1)}, u32[]{:S(2)}) copy-start(bf16[2048,128]{1,0:T(8,128)(2,1)} %param.9) | copy-start | bytes 1572868
  6.5 80.9 %all-gather.3.cloned.1.call-start = ((), (), s32[]{:S(2)}) async-start(), calls=%async_computation.4 | async-start | bytes 5570560 | tf_op jit(solution)/shard_map/all_gather | solution.py:48
  7.3 174.7 %reduce-scatter.2.cloned.1.call-start = ((), (), s32[]{:S(2)}) async-start(), calls=%async_computation.5 | async-start | bytes 2088960 | tf_op jit(solution)/shard_map/reduce_scatter | solution.py:57
  94.1 139.1 %copy-start.1 = (bf16[1,128,768]{2,1,0:T(8,128)(2,1)S(1)}, bf16[1,128,768]{2,1,0:T(8,128)(2,1)}, u32[]{:S(2)}) copy-start(bf16[1,128,768]{2,1,0:T(8,128)(2,1)} %param.11) | copy-start | bytes 589828
  94.1 140.0 %copy-start.2 = (s32[1,128]{1,0:T(1,128)S(1)}, s32[1,128]{1,0:T(1,128)}, u32[]{:S(2)}) copy-start(s32[1,128]{1,0:T(1,128)} %param.15) | copy-start | bytes 1540
  94.1 210.9 %copy-start.3 = (s32[1,128]{1,0:T(1,128)S(1)}, s32[1,128]{1,0:T(1,128)}, u32[]{:S(2)}) copy-start(s32[1,128]{1,0:T(1,128)} %param.14) | copy-start | bytes 1540
  94.1 210.8 %all-gather.5.cloned.1.call-start = ((), (), s32[]{:S(2)}) async-start(), calls=%async_computation.6 | async-start | bytes 4177920 | tf_op jit(solution)/shard_map/all_gather | solution.py:74
  229.3 15.8 %all-to-all-start = ((s32[32,5,1]{1,2,0:T(1,128)}), s32[32,5,1]{1,2,0:T(1,128)S(1)}, u32[]{:S(2)}, u32[]{:S(2)}) async-start(s32[32,5,1]{1,2,0:T(1,128)} %bitcast.5), calls=%async_computation | async-start | bytes 32768 | tf_op jit(solution)/shard_map/all_to_all | solution.py:71
  365.2 44.0 %all-to-all-start.2 = ((f32[32,5,1]{1,2,0:T(1,128)}), f32[32,5,1]{1,2,0:T(1,128)S(1)}, u32[]{:S(2)}, u32[]{:S(2)}) async-start(f32[32,5,1]{1,2,0:T(1,128)} %bitcast.9), calls=%async_computation.3 | async-start | bytes 32768 | tf_op jit(solution)/shard_map/all_to_all | solution.py:80
Sparse Core Ops, SparseCore 0:
  10.4 76.9 all-gather.2
  94.2 87.7 reduce-scatter.1
  227.8 55.1 all-gather.4
where the time goes:
time: 419 us
  waiting for transfers between devices  188 us (45%)
  blocking collectives  157 us (37%)
  starting transfers between devices  36.1 us (9%)
  between operations  13.9 us (3%)
  matrix products  11.4 us (3%)
  local copies, waits for them, and re-layouts  7.26 us (2%)
  other arithmetic  5.84 us (1%)
    reduce_scatter x1, waiting for transfers between devices, body(): lax.psum_scatter(jnp.dot(hidden, w_embed, preferred_element_type=jnp.floa...  85.9 us
    all_gather x1, waiting for transfers between devices, body(): lax.all_gather(features, 'tensor', axis=0, tiled=True)  80.1 us
    unnamed x1, blocking collectives  58.3 us
    pmax x1, blocking collectives, body(): merged = lax.pmax(partial_value, 'tensor')  55.9 us
    all_to_all x1, blocking collectives, body(): lax.all_to_all(outgoing, 'dp', split_axis=0, concat_axis=0, tiled=True)  42.5 us
    all_to_all x1, starting transfers between devices, body(): lax.all_to_all(own_best, 'dp', split_axis=0, concat_axis=0, tiled=True)  32.1 us
    all_to_all x1, waiting for transfers between devices, body(): lax.all_to_all(own_best, 'dp', split_axis=0, concat_axis=0, tiled=True)  11.9 us
    all_to_all x1, waiting for transfers between devices, body(): lax.all_to_all(slot_tag, 'dp', split_axis=0, concat_axis=0, tiled=True)  8.98 us
  transfers between devices with their start and end apart: 5, of which 4 were waited for; matrix products, arithmetic and copies ran while one was open for 2% of the time, Pallas kernels for 0%

commit v1 on v0

--- a/solution.py
+++ b/solution.py
@@ -4,6 +4,27 @@
 from jax.sharding import PartitionSpec as P
 
 epsilon = 1e-06
+
+
+def gather_around(array, axis, dim):
+    length, index, extent = (lax.axis_size(axis), lax.axis_index(axis), array.shape[dim])
+    ahead = [(i, (i + 1) % length) for i in range(length)]
+    left = [(i, (i - 1) % length) for i in range(length)]
+    out = jnp.zeros((*array.shape[:dim], length * extent, *array.shape[dim + 1 :]), array.dtype)
+    out = lax.dynamic_update_slice_in_dim(out, array, index * extent, axis=dim)
+    from_left = from_right = array
+    middle = length // 2
+    for hop in range(1, middle + 1):
+        from_left = lax.ppermute(from_left, axis, ahead)
+        out = lax.dynamic_update_slice_in_dim(
+            out, from_left, (index - hop) % length * extent, axis=dim
+        )
+        if hop < length - middle:
+            from_right = lax.ppermute(from_right, axis, left)
+            out = lax.dynamic_update_slice_in_dim(
+                out, from_right, (index + hop) % length * extent, axis=dim
+            )
+    return out
 
 
 def unit_rows(vectors):
@@ -44,11 +65,7 @@
     row_total = features.shape[0]
     slot_cap = min(row_total, max(2, 2 * row_total // owners_count))
     hidden = jax.nn.gelu(
-        jnp.dot(
-            lax.all_gather(features, "tensor", axis=0, tiled=True),
-            w_hidden,
-            preferred_element_type=jnp.float32,
-        )
+        jnp.dot(gather_around(features, "tensor", 0), w_hidden, preferred_element_type=jnp.float32)
     ).astype(jnp.bfloat16)
     unit = unit_rows(members.reshape(members.shape[1], members.shape[2]))
     cluster_here = member_cluster.reshape(-1)

time: 419 us -> 444 us (1.060)
  starting transfers between devices: 36.1 us -> 100 us
  waiting for transfers between devices: 188 us -> 132 us
  local copies, waits for them, and re-layouts: 7.26 us -> 22.2 us
    all_gather x1 -> x0, waiting for transfers between devices: 80.1 us -> none  [body(): lax.all_gather(features, 'tensor', axis=0, tiled=True)]
    ppermute x0 -> x15, starting transfers between devices: none -> 64.3 us  [the longest x7 46.9 us: gather_around(): from_right = lax.ppermute(from_right, axis, left)]
    ppermute x0 -> x15, waiting for transfers between devices: none -> 23.4 us  [the longest x8 22.8 us: gather_around(): from_left = lax.ppermute(from_left, axis, ahead)]
    dynamic_update_slice x0 -> x16, local copies, waits for them, and re-layouts: none -> 12 us  [the longest x8 6.04 us: gather_around(): lax.dynamic_update_slice_in_dim(out, from_left, (index - hop) % length *...]
  transfers between devices with their start and end apart: 5 -> 19, of which waited for: 4 -> 12; matrix products, arithmetic and copies ran while one was open for 2% -> 5% of each run, Pallas kernels for 0% -> 0%
where the time goes in v1:
time: 444 us; the launch traced here: 443 us
  blocking collectives  157 us (35%)
  waiting for transfers between devices  132 us (30%)
  starting transfers between devices  100 us (23%)
  local copies, waits for them, and re-layouts  22.2 us (5%)
  between operations  14.7 us (3%)
  matrix products  11.4 us (3%)
  other arithmetic  5.84 us (1%)
    reduce_scatter x1, waiting for transfers between devices, body(): lax.psum_scatter(jnp.dot(hidden, w_embed, preferred_element_type=jnp.floa...  87.5 us
    unnamed x1, blocking collectives  58.3 us
    pmax x1, blocking collectives, body(): merged = lax.pmax(partial_value, 'tensor')  55.9 us
    ppermute x7, starting transfers between devices, gather_around(): from_right = lax.ppermute(from_right, axis, left)  46.9 us
    all_to_all x1, blocking collectives, body(): lax.all_to_all(outgoing, 'dp', split_axis=0, concat_axis=0, tiled=True)  42.5 us
    all_to_all x1, starting transfers between devices, body(): lax.all_to_all(own_best, 'dp', split_axis=0, concat_axis=0, tiled=True)  32.1 us
    ppermute x8, waiting for transfers between devices, gather_around(): from_left = lax.ppermute(from_left, axis, ahead)  22.8 us
    ppermute x8, starting transfers between devices, gather_around(): from_left = lax.ppermute(from_left, axis, ahead)  17.4 us
  transfers between devices with their start and end apart: 19, of which 12 were waited for; matrix products, arithmetic and copies ran while one was open for 5% of the time, Pallas kernels for 0%

profile of v1, /device:TPU:1, one launch (start us, length us, event | category | flops | bytes accessed | tf_op | source)
XLA Modules:
  0.0 443.0 jit_solution(2216455451812724818)
XLA Ops:
  6.5 4.1 collective-permute-start
  10.6 5.6 %collective-permute-start.1 = (bf16[80,2048]{1,0:T(8,128)(2,1)}, bf16[80,2048]{1,0:T(8,128)(2,1)S(1)}, u32[]{:S(2)}, u32[]{:S(2)}) collective-permute-start(bf16[80,2048]{1,0:T(8,128)(2,1)} %param.8), channel_id=1, source_target_pairs={{0,15},{1,0},{2,1},{3,2},{4,3},{5,4},{6,5},{7,6},{8,7},{9,8},{10,9... | collective-permute-start | bytes 983048 | tf_op jit(solution)/shard_map/ppermute | solution.py:23
  16.5 3.0 broadcast_in_dim.35
  20.3 1.9 collective-permute-start.2
  22.2 6.7 %collective-permute-start.3 = (bf16[80,2048]{1,0:T(8,128)(2,1)S(1)}, bf16[80,2048]{1,0:T(8,128)(2,1)S(1)}, u32[]{:S(2)}, u32[]{:S(2)}) collective-permute-start(bf16[80,2048]{1,0:T(8,128)(2,1)S(1)} %collective-permute-done.1), channel_id=1, source_target_pairs={{0,15},{1,0},{2,1},{3,2},{4,3},{5,4},{6,5},{7,6},{8,7},{9,8},{10,9... | collective-permute-start | bytes 983048 | tf_op jit(solution)/shard_map/ppermute | solution.py:23
  31.4 1.9 collective-permute-start.4
  33.3 6.7 %collective-permute-start.5 = (bf16[80,2048]{1,0:T(8,128)(2,1)S(1)}, bf16[80,2048]{1,0:T(8,128)(2,1)S(1)}, u32[]{:S(2)}, u32[]{:S(2)}) collective-permute-start(bf16[80,2048]{1,0:T(8,128)(2,1)S(1)} %collective-permute-done.3), channel_id=1, source_target_pairs={{0,15},{1,0},{2,1},{3,2},{4,3},{5,4},{6,5},{7,6},{8,7},{9,8},{10,9... | collective-permute-start | bytes 983048 | tf_op jit(solution)/shard_map/ppermute | solution.py:23
  42.5 1.9 collective-permute-start.6
  44.4 6.7 %collective-permute-start.7 = (bf16[80,2048]{1,0:T(8,128)(2,1)S(1)}, bf16[80,2048]{1,0:T(8,128)(2,1)S(1)}, u32[]{:S(2)}, u32[]{:S(2)}) collective-permute-start(bf16[80,2048]{1,0:T(8,128)(2,1)S(1)} %collective-permute-done.5), channel_id=1, source_target_pairs={{0,15},{1,0},{2,1},{3,2},{4,3},{5,4},{6,5},{7,6},{8,7},{9,8},{10,9... | collective-permute-start | bytes 983048 | tf_op jit(solution)/shard_map/ppermute | solution.py:23
  52.6 1.4 collective-permute-done.6
  54.1 1.9 collective-permute-start.8
  56.0 7.0 %collective-permute-start.9 = (bf16[80,2048]{1,0:T(8,128)(2,1)S(1)}, bf16[80,2048]{1,0:T(8,128)(2,1)S(1)}, u32[]{:S(2)}, u32[]{:S(2)}) collective-permute-start(bf16[80,2048]{1,0:T(8,128)(2,1)S(1)} %collective-permute-done.7), channel_id=1, source_target_pairs={{0,15},{1,0},{2,1},{3,2},{4,3},{5,4},{6,5},{7,6},{8,7},{9,8},{10,9... | collective-permute-start | bytes 983048 | tf_op jit(solution)/shard_map/ppermute | solution.py:23
  64.5 2.2 collective-permute-done.8
  66.7 1.9 collective-permute-start.10
  68.8 7.1 %collective-permute-start.11 = (bf16[80,2048]{1,0:T(8,128)(2,1)S(1)}, bf16[80,2048]{1,0:T(8,128)(2,1)S(1)}, u32[]{:S(2)}, u32[]{:S(2)}) collective-permute-start(bf16[80,2048]{1,0:T(8,128)(2,1)S(1)} %collective-permute-done.9), channel_id=1, source_target_pairs={{0,15},{1,0},{2,1},{3,2},{4,3},{5,4},{6,5},{7,6},{8,7},{9,8},{10,9... | collective-permute-start | bytes 983048 | tf_op jit(solution)/shard_map/ppermute | solution.py:23
  77.4 3.1 collective-permute-done.10
  80.5 1.9 collective-permute-start.12
  82.8 7.1 %collective-permute-start.13 = (bf16[80,2048]{1,0:T(8,128)(2,1)S(1)}, bf16[80,2048]{1,0:T(8,128)(2,1)S(1)}, u32[]{:S(2)}, u32[]{:S(2)}) collective-permute-start(bf16[80,2048]{1,0:T(8,128)(2,1)S(1)} %collective-permute-done.11), channel_id=1, source_target_pairs={{0,15},{1,0},{2,1},{3,2},{4,3},{5,4},{6,5},{7,6},{8,7},{9,8},{10,9... | collective-permute-start | bytes 983048 | tf_op jit(solution)/shard_map/ppermute | solution.py:23
  91.5 3.7 collective-permute-done.12
  95.2 1.9 collective-permute-start.14
  98.6 10.4 %collective-permute-done.14 = bf16[80,2048]{1,0:T(8,128)(2,1)S(1)} collective-permute-done((bf16[80,2048]{1,0:T(8,128)(2,1)S(1)}, bf16[80,2048]{1,0:T(8,128)(2,1)S(1)}, u32[]{:S(2)}, u32[]{:S(2)}) %collective-permute-start.14) | collective-permute-done | bytes 327712 | tf_op jit(solution)/shard_map/ppermute | solution.py:18
  109.7 6.7 %convolution_convert_fusion = bf16[1280,768]{1,0:T(8,128)(2,1)} fusion(bf16[128,768]{1,0:T(8,128)(2,1)S(1)} %copy-done.3, bf16[1280,2048]{1,0:T(8,128)(2,1)} %constant_dynamic-update-slice_fusion, bf16[2048,128]{1,0:T(8,128)(2,1)S(1)} %copy-done), kind=kOutput, calls=%fused_computation.2 | convolution fusion | flops 925204480 | bytes 7929856 | tf_op jit(solution)/shard_map/dot_general | solution.py:75
  118.4 87.5 %reduce-scatter.2.cloned.1.call-done = bf16[80,768]{1,0:T(8,128)(2,1)} async-done(((bf16[1280,768]{1,0:T(8,128)(2,1)}), bf16[80,768]{1,0:T(8,128)(2,1)}) %reduce-scatter.2.cloned.1.call-update) | async-done | bytes 122896 | tf_op jit(solution)/shard_map/reduce_scatter | solution.py:74
  208.3 42.5 %all_to_all.36 = bf16[32,5,768]{2,1,0:T(8,128)(2,1)S(1)} all-to-all(bf16[32,5,768]{2,1,0:T(8,128)(2,1)S(1)} %all_to_all.27), channel_id=1, replica_groups=mesh['dp'=32,'tensor'=16] {'dp'}, dimensions={0} | all-to-all | bytes 491520 | tf_op jit(solution)/shard_map/all_to_all | solution.py:87
  253.2 3.9 all-to-all-start
  258.0 1.3 dynamic-slice.1
  260.0 9.0 %all-to-all-done = s32[32,5,1]{1,2,0:T(1,128)S(1)} async-done(((s32[32,5,1]{1,2,0:T(1,128)}), s32[32,5,1]{1,2,0:T(1,128)S(1)}, u32[]{:S(2)}, u32[]{:S(2)}) %all-to-all-start) | async-done | bytes 672 | tf_op jit(solution)/shard_map/all_to_all | solution.py:88
  270.6 58.3 %all-reduce = s32[2560]{0:T(1024)S(1)} all-reduce(s32[2560]{0:T(1024)S(1)} %dynamic-update-slice), channel_id=1, replica_groups=mesh['dp'=32,'tensor'=16] {'tensor'}, use_global_device_ids=true, to_apply=%add | all-reduce | flops 2560 | bytes 20480
  328.9 3.5 fusion
  332.4 55.9 %pmax.7 = f32[2560]{0:T(1024)S(1)} all-reduce(f32[2560]{0:T(1024)S(1)} %fusion), channel_id=1, replica_groups=mesh['dp'=32,'tensor'=16] {'tensor'}, use_global_device_ids=true, to_apply=%region_7.8 | all-reduce | flops 2560 | bytes 20480 | tf_op jit(solution)/shard_map/pmax | solution.py:95
  389.1 32.1 %all-to-all-start.2 = ((f32[32,5,1]{1,2,0:T(1,128)}), f32[32,5,1]{1,2,0:T(1,128)S(1)}, u32[]{:S(2)}, u32[]{:S(2)}) async-start(f32[32,5,1]{1,2,0:T(1,128)} %bitcast.9), calls=%async_computation.3 | async-start | bytes 32768 | tf_op jit(solution)/shard_map/all_to_all | solution.py:97
  421.2 11.9 %all-to-all-done.2 = f32[32,5,1]{1,2,0:T(1,128)S(1)} async-done(((f32[32,5,1]{1,2,0:T(1,128)}), f32[32,5,1]{1,2,0:T(1,128)S(1)}, u32[]{:S(2)}, u32[]{:S(2)}) %all-to-all-start.2) | async-done | bytes 672 | tf_op jit(solution)/shard_map/all_to_all | solution.py:97
  (74 shorter events, 27.7 us)
Async XLA Ops:
  6.5 103.2 %copy-start = (bf16[2048,128]{1,0:T(8,128)(2,1)S(1)}, bf16[2048,128]{1,0:T(8,128)(2,1)}, u32[]{:S(2)}) copy-start(bf16[2048,128]{1,0:T(8,128)(2,1)} %param.9) | copy-start | bytes 1572868
  6.5 13.0 %copy-start.1 = (bf16[80,2048]{1,0:T(8,128)(2,1)S(1)}, bf16[80,2048]{1,0:T(8,128)(2,1)}, u32[]{:S(2)}) copy-start(bf16[80,2048]{1,0:T(8,128)(2,1)} %param.8) | copy-start | bytes 983044
  6.5 199.4 %reduce-scatter.2.cloned.1.call-start = ((), (), s32[]{:S(2)}) async-start(), calls=%async_computation.4 | async-start | bytes 2088960 | tf_op jit(solution)/shard_map/reduce_scatter | solution.py:74
  6.5 13.7 %collective-permute-start = (bf16[80,2048]{1,0:T(8,128)(2,1)}, bf16[80,2048]{1,0:T(8,128)(2,1)S(1)}, u32[]{:S(2)}, u32[]{:S(2)}) collective-permute-start(bf16[80,2048]{1,0:T(8,128)(2,1)} %param.8), channel_id=1, source_target_pairs={{0,1},{1,2},{2,3},{3,4},{4,5},{5,6},{6,7},{7,8},{8,9},{9,10},{10,1... | collective-permute-start | bytes 983048 | tf_op jit(solution)/shard_map/ppermute | solution.py:18
  10.6 11.6 %collective-permute-start.1 = (bf16[80,2048]{1,0:T(8,128)(2,1)}, bf16[80,2048]{1,0:T(8,128)(2,1)S(1)}, u32[]{:S(2)}, u32[]{:S(2)}) collective-permute-start(bf16[80,2048]{1,0:T(8,128)(2,1)} %param.8), channel_id=1, source_target_pairs={{0,15},{1,0},{2,1},{3,2},{4,3},{5,4},{6,5},{7,6},{8,7},{9,8},{10,9... | collective-permute-start | bytes 983048 | tf_op jit(solution)/shard_map/ppermute | solution.py:23
  19.5 90.2 %copy-start.3 = (bf16[128,768]{1,0:T(8,128)(2,1)S(1)}, bf16[128,768]{1,0:T(8,128)(2,1)}, u32[]{:S(2)}) copy-start(bf16[128,768]{1,0:T(8,128)(2,1)} %param.10) | copy-start | bytes 589828
  20.3 11.1 %collective-permute-start.2 = (bf16[80,2048]{1,0:T(8,128)(2,1)S(1)}, bf16[80,2048]{1,0:T(8,128)(2,1)S(1)}, u32[]{:S(2)}, u32[]{:S(2)}) collective-permute-start(bf16[80,2048]{1,0:T(8,128)(2,1)S(1)} %collective-permute-done), channel_id=1, source_target_pairs={{0,1},{1,2},{2,3},{3,4},{4,5},{5,6},{6,7},{7,8},{8,9},{9,10},{10,1... | collective-permute-start | bytes 983048 | tf_op jit(solution)/shard_map/ppermute | solution.py:18
  22.2 11.1 %collective-permute-start.3 = (bf16[80,2048]{1,0:T(8,128)(2,1)S(1)}, bf16[80,2048]{1,0:T(8,128)(2,1)S(1)}, u32[]{:S(2)}, u32[]{:S(2)}) collective-permute-start(bf16[80,2048]{1,0:T(8,128)(2,1)S(1)} %collective-permute-done.1), channel_id=1, source_target_pairs={{0,15},{1,0},{2,1},{3,2},{4,3},{5,4},{6,5},{7,6},{8,7},{9,8},{10,9... | collective-permute-start | bytes 983048 | tf_op jit(solution)/shard_map/ppermute | solution.py:23
  31.4 11.1 %collective-permute-start.4 = (bf16[80,2048]{1,0:T(8,128)(2,1)S(1)}, bf16[80,2048]{1,0:T(8,128)(2,1)S(1)}, u32[]{:S(2)}, u32[]{:S(2)}) collective-permute-start(bf16[80,2048]{1,0:T(8,128)(2,1)S(1)} %collective-permute-done.2), channel_id=1, source_target_pairs={{0,1},{1,2},{2,3},{3,4},{4,5},{5,6},{6,7},{7,8},{8,9},{9,10},{10,1... | collective-permute-start | bytes 983048 | tf_op jit(solution)/shard_map/ppermute | solution.py:18
  33.3 11.1 %collective-permute-start.5 = (bf16[80,2048]{1,0:T(8,128)(2,1)S(1)}, bf16[80,2048]{1,0:T(8,128)(2,1)S(1)}, u32[]{:S(2)}, u32[]{:S(2)}) collective-permute-start(bf16[80,2048]{1,0:T(8,128)(2,1)S(1)} %collective-permute-done.3), channel_id=1, source_target_pairs={{0,15},{1,0},{2,1},{3,2},{4,3},{5,4},{6,5},{7,6},{8,7},{9,8},{10,9... | collective-permute-start | bytes 983048 | tf_op jit(solution)/shard_map/ppermute | solution.py:23
  42.5 11.6 %collective-permute-start.6 = (bf16[80,2048]{1,0:T(8,128)(2,1)S(1)}, bf16[80,2048]{1,0:T(8,128)(2,1)S(1)}, u32[]{:S(2)}, u32[]{:S(2)}) collective-permute-start(bf16[80,2048]{1,0:T(8,128)(2,1)S(1)} %collective-permute-done.4), channel_id=1, source_target_pairs={{0,1},{1,2},{2,3},{3,4},{4,5},{5,6},{6,7},{7,8},{8,9},{9,10},{10,1... | collective-permute-start | bytes 983048 | tf_op jit(solution)/shard_map/ppermute | solution.py:18
  44.4 11.6 %collective-permute-start.7 = (bf16[80,2048]{1,0:T(8,128)(2,1)S(1)}, bf16[80,2048]{1,0:T(8,128)(2,1)S(1)}, u32[]{:S(2)}, u32[]{:S(2)}) collective-permute-start(bf16[80,2048]{1,0:T(8,128)(2,1)S(1)} %collective-permute-done.5), channel_id=1, source_target_pairs={{0,15},{1,0},{2,1},{3,2},{4,3},{5,4},{6,5},{7,6},{8,7},{9,8},{10,9... | collective-permute-start | bytes 983048 | tf_op jit(solution)/shard_map/ppermute | solution.py:23
  54.1 12.7 %collective-permute-start.8 = (bf16[80,2048]{1,0:T(8,128)(2,1)S(1)}, bf16[80,2048]{1,0:T(8,128)(2,1)S(1)}, u32[]{:S(2)}, u32[]{:S(2)}) collective-permute-start(bf16[80,2048]{1,0:T(8,128)(2,1)S(1)} %collective-permute-done.6), channel_id=1, source_target_pairs={{0,1},{1,2},{2,3},{3,4},{4,5},{5,6},{6,7},{7,8},{8,9},{9,10},{10,1... | collective-permute-start | bytes 983048 | tf_op jit(solution)/shard_map/ppermute | solution.py:18
  56.0 12.8 %collective-permute-start.9 = (bf16[80,2048]{1,0:T(8,128)(2,1)S(1)}, bf16[80,2048]{1,0:T(8,128)(2,1)S(1)}, u32[]{:S(2)}, u32[]{:S(2)}) collective-permute-start(bf16[80,2048]{1,0:T(8,128)(2,1)S(1)} %collective-permute-done.7), channel_id=1, source_target_pairs={{0,15},{1,0},{2,1},{3,2},{4,3},{5,4},{6,5},{7,6},{8,7},{9,8},{10,9... | collective-permute-start | bytes 983048 | tf_op jit(solution)/shard_map/ppermute | solution.py:23
  66.7 13.7 %collective-permute-start.10 = (bf16[80,2048]{1,0:T(8,128)(2,1)S(1)}, bf16[80,2048]{1,0:T(8,128)(2,1)S(1)}, u32[]{:S(2)}, u32[]{:S(2)}) collective-permute-start(bf16[80,2048]{1,0:T(8,128)(2,1)S(1)} %collective-permute-done.8), channel_id=1, source_target_pairs={{0,1},{1,2},{2,3},{3,4},{4,5},{5,6},{6,7},{7,8},{8,9},{9,10},{10,1... | collective-permute-start | bytes 983048 | tf_op jit(solution)/shard_map/ppermute | solution.py:18
  68.8 14.0 %collective-permute-start.11 = (bf16[80,2048]{1,0:T(8,128)(2,1)S(1)}, bf16[80,2048]{1,0:T(8,128)(2,1)S(1)}, u32[]{:S(2)}, u32[]{:S(2)}) collective-permute-start(bf16[80,2048]{1,0:T(8,128)(2,1)S(1)} %collective-permute-done.9), channel_id=1, source_target_pairs={{0,15},{1,0},{2,1},{3,2},{4,3},{5,4},{6,5},{7,6},{8,7},{9,8},{10,9... | collective-permute-start | bytes 983048 | tf_op jit(solution)/shard_map/ppermute | solution.py:23
  80.5 14.7 %collective-permute-start.12 = (bf16[80,2048]{1,0:T(8,128)(2,1)S(1)}, bf16[80,2048]{1,0:T(8,128)(2,1)S(1)}, u32[]{:S(2)}, u32[]{:S(2)}) collective-permute-start(bf16[80,2048]{1,0:T(8,128)(2,1)S(1)} %collective-permute-done.10), channel_id=1, source_target_pairs={{0,1},{1,2},{2,3},{3,4},{4,5},{5,6},{6,7},{7,8},{8,9},{9,10},{10,1... | collective-permute-start | bytes 983048 | tf_op jit(solution)/shard_map/ppermute | solution.py:18
  82.8 15.0 %collective-permute-start.13 = (bf16[80,2048]{1,0:T(8,128)(2,1)S(1)}, bf16[80,2048]{1,0:T(8,128)(2,1)S(1)}, u32[]{:S(2)}, u32[]{:S(2)}) collective-permute-start(bf16[80,2048]{1,0:T(8,128)(2,1)S(1)} %collective-permute-done.11), channel_id=1, source_target_pairs={{0,15},{1,0},{2,1},{3,2},{4,3},{5,4},{6,5},{7,6},{8,7},{9,8},{10,9... | collective-permute-start | bytes 983048 | tf_op jit(solution)/shard_map/ppermute | solution.py:23
  95.2 13.8 %collective-permute-start.14 = (bf16[80,2048]{1,0:T(8,128)(2,1)S(1)}, bf16[80,2048]{1,0:T(8,128)(2,1)S(1)}, u32[]{:S(2)}, u32[]{:S(2)}) collective-permute-start(bf16[80,2048]{1,0:T(8,128)(2,1)S(1)} %collective-permute-done.12), channel_id=1, source_target_pairs={{0,1},{1,2},{2,3},{3,4},{4,5},{5,6},{6,7},{7,8},{8,9},{9,10},{10,1... | collective-permute-start | bytes 983048 | tf_op jit(solution)/shard_map/ppermute | solution.py:18
  109.7 147.4 %copy-start.2 = (bf16[1,128,768]{2,1,0:T(8,128)(2,1)S(1)}, bf16[1,128,768]{2,1,0:T(8,128)(2,1)}, u32[]{:S(2)}) copy-start(bf16[1,128,768]{2,1,0:T(8,128)(2,1)} %param.11) | copy-start | bytes 589828
  109.7 148.3 %copy-start.4 = (s32[1,128]{1,0:T(1,128)S(1)}, s32[1,128]{1,0:T(1,128)}, u32[]{:S(2)}) copy-start(s32[1,128]{1,0:T(1,128)} %param.15) | copy-start | bytes 1540
  109.7 219.1 %copy-start.5 = (s32[1,128]{1,0:T(1,128)S(1)}, s32[1,128]{1,0:T(1,128)}, u32[]{:S(2)}) copy-start(s32[1,128]{1,0:T(1,128)} %param.14) | copy-start | bytes 1540
  116.4 212.4 %all-gather.2.cloned.1.call-start = ((), (), s32[]{:S(2)}) async-start(), calls=%async_computation.5 | async-start | bytes 4177920 | tf_op jit(solution)/shard_map/all_gather | solution.py:91
  253.2 15.8 %all-to-all-start = ((s32[32,5,1]{1,2,0:T(1,128)}), s32[32,5,1]{1,2,0:T(1,128)S(1)}, u32[]{:S(2)}, u32[]{:S(2)}) async-start(s32[32,5,1]{1,2,0:T(1,128)} %bitcast.5), calls=%async_computation | async-start | bytes 32768 | tf_op jit(solution)/shard_map/all_to_all | solution.py:88
  389.1 44.0 %all-to-all-start.2 = ((f32[32,5,1]{1,2,0:T(1,128)}), f32[32,5,1]{1,2,0:T(1,128)S(1)}, u32[]{:S(2)}, u32[]{:S(2)}) async-start(f32[32,5,1]{1,2,0:T(1,128)} %bitcast.9), calls=%async_computation.3 | async-start | bytes 32768 | tf_op jit(solution)/shard_map/all_to_all | solution.py:97
Sparse Core Ops, SparseCore 0:
  116.6 89.3 reduce-scatter.1
  251.7 55.0 all-gather.1
